TPU v7x, 128 devices: a whole 4x4x4 slice. The times are simulated.
128 devices in a mesh: gx: 4 (over x), gy: 4 (over z_lo, core), gz: 8 (over z_hi, y).
Axes of the slice: x: 4, y: 4, z: 4 (z_hi: 2, z_lo: 2; z = z_hi * 2 + z_lo), core: 2. Of those that a mesh axis runs over, the one named last changes fastest.
Arguments:
- orbitals: float32 [16, 32, 64, 512], P(None, 'gz', 'gy', 'gx'), may hold values from -6 to 6
- potential: float32 [32, 64, 512], P('gz', 'gy', 'gx'), may hold values from -1 to 0.5
- tile_proj: float32 [32768, 4, 128], P(('gx', 'gy', 'gz')), may hold values from -1 to 1
- tile_atom: int32 [32768], P(('gx', 'gy', 'gz')), may hold values from 0 to 8191, as said below
- tile_column: int32 [32768], P(('gx', 'gy', 'gz')), may hold values from 0 to 63
- tile_count: int32 [128], P(('gx', 'gy', 'gz')), may hold values from 64 to 256, as said below
- atom_home: int32 [8192], replicated, may hold values from 0 to 8191, each once
- coupling: float32 [8192, 4], P(('gx', 'gy', 'gz')), may hold values from 0.5 to 3
Outputs:
- filtered: float32 [16, 32, 64, 512], P(None, 'gz', 'gy', 'gx')
Inputs may be any that keep to these rules, and one draw needn't show every extreme that they name: `tile_atom`: each live or dead slot names an atom numbered d * 64 to d * 64 + 63 for a device d whose gx, gy and gz indices each differ from the slot's own device's by at most one. `tile_count`: some device has all 256 slots live. `atom_home`: each coupling row once.
All inputs are finite; a program needn't handle non-finite values.
Results may differ from a plain program's by a relative error of at most 0.00018.
Values sent between devices are 32-bit elements; how exact they have to be, the bound alone decides.
A program may use at most 128 MiB of HBM per device.

v0:
```python
import jax
import jax.numpy as jnp
import numpy as np
from jax import lax
from jax.experimental import pallas as pl
from jax.experimental.pallas import tpu as pltpu
from jax.sharding import PartitionSpec as P

F32, BF16, I32 = jnp.float32, jnp.bfloat16, jnp.int32
STENCIL = (-205.0 / 72.0, 8.0 / 5.0, -1.0 / 5.0, 8.0 / 315.0, -1.0 / 560.0)
CENTER, HALF = 14.0, 10.0
STEPS = 4
DIRS = [(dx, dy) for dx in (-1, 0, 1) for dy in (-1, 0, 1)]
SELF = 4
XP, XM, YL, YH, ZH, RS0, RO0, BS0, BO0, NSEM = 0, 1, 2, 3, 4, 5, 14, 23, 32, 41
V0, PF0, PT0, ME0, CP0, PA0, OU0, FT0, NSET = 0, 6, 12, 15, 18, 28, 31, 37, 40


def stencil_constants():
    table = np.zeros((144, 128), np.float32)
    for x in range(128):
        for k in range(1, 5):
            if x + k < 128:
                table[x, x + k] = -0.5 * STENCIL[k]
            if x - k >= 0:
                table[x, x - k] = -0.5 * STENCIL[k]
    for j in range(4):
        table[128 + j, 124 + j] = 1.0
        table[132 + j, j] = 1.0
        for x in range(128):
            k = x + 4 - j
            if 1 <= k <= 4:
                table[136 + j, x] = -0.5 * STENCIL[k]
            k = 128 + j - x
            if 1 <= k <= 4:
                table[140 + j, x] = -0.5 * STENCIL[k]
    return table


def split(value):
    high = value.astype(BF16)
    return high, (value - high.astype(F32)).astype(BF16)


def dot_nt(a, b):
    return lax.dot_general(a, b, (((1,), (1,)), ((), ())), preferred_element_type=F32)


def dot_nn(a, b):
    return lax.dot_general(a, b, (((1,), (0,)), ((), ())), preferred_element_type=F32)


def dot_tn(a, b):
    return lax.dot_general(a, b, (((0,), (0,)), ((), ())), preferred_element_type=F32)


def kernel(
    orb, pot_in, tp, atom_hbm, column_hbm, count_in, home_hbm, cpl_hbm, table_hbm, out,
    X, Z, VH, VL, PF, PT, POT, META, MKB, NIDX, NMB, WT, LH, LHO, LSA, LSO, RS, RO, CS, CSO, SSA, SSO, SHA, SHO, SC, XS, XR, CB, CONST,
    PART, PART0, PTS, PTR, ZO, ORB, RL, RLO, atom_in, column_in, home_in, cpl_in, table,
    set_s, set_r, sem_s, sem_r, local_sem,
):
    ix, iy, iz = lax.axis_index("gx"), lax.axis_index("gy"), lax.axis_index("gz")
    zh, q = iz // 4, iz % 4
    oz = 1 - zh
    edge_block = 3 * oz
    below, above, across = (q + 3) % 4, (q + 1) % 4, (q + 2) % 4

    def dev(gx, gy, gz):
        return {"gx": gx, "gy": gy, "gz": gz}

    def ring(j):
        return dev(ix, iy, zh * 4 + (q + j) % 4)

    def near(dx, dy, half):
        return dev((ix + dx + 4) % 4, (iy + dy + 4) % 4, half * 4 + q)

    def exists(i):
        dx, dy = DIRS[i]
        return jnp.logical_and(
            jnp.logical_and(ix + dx >= 0, ix + dx <= 3), jnp.logical_and(iy + dy >= 0, iy + dy <= 3)
        )

    def copy(src, dst, s, r, to):
        return pltpu.make_async_remote_copy(
            src_ref=src, dst_ref=dst, send_sem=s, recv_sem=r, device_id=to, device_id_type=pl.DeviceIdType.MESH
        )

    barrier = pltpu.get_barrier_semaphore()
    peers = [near(dx, dy, half) for dx, dy in DIRS for half in (zh, oz)]
    peers = [p for i, p in enumerate(peers) if i != 2 * SELF]
    peers += [ring(j) for j in (1, 2, 3)]
    peers += [dev((ix + 2) % 4, iy, iz), dev(ix, (iy + 2) % 4, iz)]
    for peer in peers:
        pl.semaphore_signal(barrier, inc=1, device_id=peer, device_id_type=pl.DeviceIdType.MESH)
    take_proj = pltpu.make_async_copy(tp, PF, local_sem.at[0])
    take_orb = pltpu.make_async_copy(orb, ORB, local_sem.at[1])
    take_pot = pltpu.make_async_copy(pot_in, POT.at[pl.ds(4 * q, 4)], local_sem.at[2])
    take_own = pltpu.make_async_copy(
        orb.at[pl.ds(4 * q, 4)], X.at[1, :, pl.ds(4 + 4 * q, 4), pl.ds(8, 16), :], local_sem.at[3]
    )
    smalls = [
        pltpu.make_async_copy(src, dst, local_sem.at[4 + i])
        for i, (src, dst) in enumerate(
            (
                (atom_hbm, atom_in),
                (column_hbm, column_in),
                (cpl_hbm, cpl_in),
                (table_hbm, table),
                (home_hbm.at[pl.ds(2 * ((ix * 4 + iy) * 2 + zh), 2)], home_in),
            )
        )
    ]
    for c in smalls + [take_proj, take_orb, take_own, take_pot]:
        c.start()
    for c in smalls:
        c.wait()

    atom = atom_in[...]
    owner = lax.shift_right_logical(atom, 6)
    dx = lax.shift_right_logical(owner, 5) - ix + 1
    dy = jnp.bitwise_and(lax.shift_right_logical(owner, 3), 3) - iy + 1
    zb = jnp.bitwise_and(owner, 7) - 4 * zh
    pair = jnp.where(jnp.logical_and(zb >= 0, zb < 4), lax.shift_right_arithmetic(zb, 1), 2)
    number = (dx * 3 + dy) * 3 + pair
    lane = jnp.bitwise_and(zb, 1) * 64 + jnp.bitwise_and(atom, 63)
    column = jnp.where(lax.broadcasted_iota(I32, (1, 256), 1) < count_in[0], column_in[...], -1)
    META[pl.ds(q, 1)] = jnp.concatenate([number, lane, column] + [column] * 5, axis=0)[None]
    cpl = cpl_in[...]
    mine = 2 * ((ix * 4 + iy) * 8 + iz)
    CB[pl.ds(mine, 2), :] = jnp.concatenate(
        [jnp.concatenate([cpl[0:1], cpl[1:2]], axis=1), jnp.concatenate([cpl[2:3], cpl[3:4]], axis=1)], axis=0
    )

    row64 = lax.broadcasted_iota(I32, (64, 256), 0)
    row128 = lax.broadcasted_iota(I32, (128, 256), 0)

    def masks(b):
        mask = jnp.where(row64 == META[b, 2:3, :], 1.0, 0.0).astype(BF16)
        MKB[b, 0:64] = mask
        MKB[b, 64:128] = mask

    masks(q)

    def clear(i, _):
        X[i, :, pl.ds(20 * zh, 4)] = jnp.zeros((4, 4, 32, 128), F32)

        @pl.when(iy == 0)
        def _():
            X[i, :, 4:20, 0:8] = jnp.zeros((4, 16, 8, 128), F32)

        @pl.when(iy == 3)
        def _():
            X[i, :, 4:20, 24:32] = jnp.zeros((4, 16, 8, 128), F32)

        return 0

    lax.fori_loop(1, 5, clear, 0)

    def clear_sums(i, _):
        for slot in range(9):
            if slot != SELF:

                @pl.when(jnp.logical_not(exists(slot)))
                def _():
                    RS[i, slot] = jnp.zeros((2, 16, 128), F32)
                    RO[i, slot] = jnp.zeros((8, 128), F32)

        return 0

    lax.fori_loop(0, 4, clear_sums, 0)

    wx_h, wx_l = split(table[0:128, :])
    CONST[0:128, 0:128] = wx_h
    CONST[0:128, 128:256] = wx_l
    e2 = table[128:136, :].astype(BF16)
    edge_row = lax.broadcasted_iota(I32, (8, 128), 0)
    inside = jnp.where(
        edge_row < 4, jnp.where(ix > 0, 1.0, 0.0).astype(F32), jnp.where(ix < 3, 1.0, 0.0).astype(F32)
    )
    edge = table[136:144, :] * inside
    edge_h = edge.astype(BF16).astype(F32)
    edge_1 = jnp.concatenate([edge_h, edge_h], axis=0).astype(BF16)
    edge_2 = jnp.concatenate([edge - edge_h, edge - edge_h], axis=0).astype(BF16)

    take_proj.wait()
    for p in range(4):
        PT[q, p] = PF[pl.ds(p, 256, stride=4), :].T
    pl.semaphore_wait(barrier, len(peers))

    def field_block(index, block):
        return X.at[index, :, pl.ds(4 + 4 * block, 4), pl.ds(8, 16), :]

    sends = []

    def start(c):
        c.start()
        sends.append(c)
        return c

    def set_copy(src, dst, index, to):
        return copy(src, dst, set_s.at[index], set_r.at[index], to)

    def rows(first, count):
        return CB.at[pl.ds(first, count)]

    metas = [start(set_copy(META.at[q], META.at[q], ME0 + j - 1, ring(j))) for j in (1, 3, 2)]
    ring_cpl = [start(set_copy(rows(mine, 2), rows(mine, 2), CP0 + j - 1, ring(j))) for j in (1, 3, 2)]

    def around(source, target, relay, base):
        to_up = start(set_copy(source(across, 0, 2), relay.at[0], base, ring(1)))
        to_down = start(set_copy(source(across, 2, 2), relay.at[1], base + 1, ring(3)))
        near_up = start(set_copy(source(above, 0, 4), target(q, 0, 4), base + 2, ring(1)))
        near_down = start(set_copy(source(below, 0, 4), target(q, 0, 4), base + 3, ring(3)))

        def forward():
            to_up.wait_recv()
            far_up = start(set_copy(relay.at[0], target(below, 0, 2), base + 4, ring(1)))
            to_down.wait_recv()
            far_down = start(set_copy(relay.at[1], target(above, 2, 2), base + 5, ring(3)))
            return near_up, near_down, far_up, far_down

        return forward

    values_on = around(
        lambda block, o, n: orb.at[pl.ds(4 * block + o, n)],
        lambda block, o, n: X.at[1, pl.ds(o, n), pl.ds(4 + 4 * block, 4), pl.ds(8, 16), :],
        RL,
        V0,
    )

    def tile_sums(vh, vl, b, result, at):
        for o in range(4):
            r = dot_tn(jnp.concatenate([vh[o], vl[o]], axis=0), MKB[b])
            for p in range(4):
                result[at, pl.ds(p * 4 + o, 1), :] = jnp.sum(r * PT[b, p], axis=0, keepdims=True)

    take_orb.wait()

    def own_sums(g, _):
        vh, vl = split(ORB[pl.ds(4 * g, 4)].reshape(4, 64, 128))
        tile_sums(vh, vl, q, PART0, g)
        return 0

    lax.fori_loop(0, 4, own_sums, 0)
    values = values_on()
    parts = [start(set_copy(PART0.at[(q + j) % 4], PART.at[q], PA0 + j - 1, ring(j))) for j in (2, 1, 3)]
    half = [pl.ds(0, 2), pl.ds(2, 2)]
    up = [start(set_copy(PT.at[q, half[h]], PT.at[q, half[h]], PF0 + h, ring(1))) for h in (0, 1)]
    down = [start(set_copy(PT.at[q, half[h]], PT.at[q, half[h]], PF0 + 3 - h, ring(3))) for h in (1, 0)]
    pots = [start(set_copy(pot_in, POT.at[pl.ds(4 * q, 4)], PT0 + j - 1, ring(j))) for j in (1, 3, 2)]
    PART[pl.ds(q, 1)] = PART0[pl.ds(q, 1)]

    for c in ring_cpl:
        c.wait_recv()
    group = 2 * ((ix * 4 + iy) * 8 + zh * 4)
    flip = start(set_copy(rows(group, 8), rows(group, 8), CP0 + 3, dev(ix, iy, oz * 4 + q)))

    for c in metas:
        c.wait_recv()
    masks(below)
    masks(above)
    masks(across)
    for b in range(4):
        index = META[b]
        hot = jnp.where(row128 == index[1:2, :], 1.0, 0.0).astype(BF16)
        WT[b, 0:128] = hot
        WT[b, 128:256] = hot
        number = jnp.broadcast_to(index[0:1, :], (16, 256))
        NIDX[b] = number
        for n in range(27):
            NMB[b, n] = jnp.where(number == n, 1.0, 0.0).astype(BF16)

    flip.wait_recv()
    group = 2 * ((ix * 4 + iy) * 8)
    cpl_y = [
        start(set_copy(rows(group, 16), rows(group, 16), CP0 + 3 + j, dev(ix, (iy + j) % 4, iz))) for j in (1, 3, 2)
    ]

    def step_copies(s):
        cur = s + 1

        def sc(src, dst, index, to):
            return copy(src, dst, sem_s.at[s, index], sem_r.at[s, index], to)

        c = {}
        c["xp"] = sc(XS.at[s, pl.ds(0, 4)], XR.at[s, pl.ds(0, 4)], XP, dev((ix + 1) % 4, iy, iz))
        c["xm"] = sc(XS.at[s, pl.ds(4, 4)], XR.at[s, pl.ds(4, 4)], XM, dev((ix + 3) % 4, iy, iz))
        inner = pl.ds(4, 16)
        c["yl"] = sc(
            X.at[cur, :, inner, pl.ds(8, 4), :], X.at[cur, :, inner, pl.ds(24, 4), :], YL, dev(ix, (iy + 3) % 4, iz)
        )
        c["yh"] = sc(
            X.at[cur, :, inner, pl.ds(20, 4), :], X.at[cur, :, inner, pl.ds(4, 4), :], YH, dev(ix, (iy + 1) % 4, iz)
        )
        c["z"] = sc(
            X.at[cur, :, pl.ds(4 + 12 * oz, 4), pl.ds(8, 16), :],
            X.at[cur, :, pl.ds(20 * zh, 4), pl.ds(8, 16), :],
            ZH,
            dev(ix, iy, oz * 4 + q),
        )
        for i, (dx, dy) in enumerate(DIRS):
            slot = 8 - i
            if i != SELF:
                c["rs", i] = sc(LSA.at[s, i], RS.at[s, slot], RS0 + slot, near(dx, dy, zh))
                c["bs", i] = sc(CS.at[s], SSA.at[s, slot], BS0 + slot, near(dx, dy, zh))
            c["ro", i] = sc(LSO.at[s, i], RO.at[s, slot], RO0 + slot, near(dx, dy, oz))
            c["bo", i] = sc(CSO.at[s], SSO.at[s, slot], BO0 + slot, near(dx, dy, oz))
        return c

    def when(condition, action):
        @pl.when(condition)
        def _():
            action()

    def neighbours(c, names, action, mirrored):
        for i in range(9):
            def both(i=i):
                for name in names:
                    if (name, i) in c:
                        getattr(c[name, i], action)()

            if i == SELF:
                both()
            else:
                when(exists(8 - i if mirrored else i), both)

    def send_y(c):
        when(iy > 0, c["yl"].start)
        when(iy < 3, c["yh"].start)

    def pack_x(s, c):
        vh_all = VH[...].reshape(1024, 128)
        vl_all = VL[...].reshape(1024, 128)
        XS[s] = dot_nt(e2, vh_all) + dot_nt(e2, vl_all)
        xp = dot_nt(jnp.concatenate([vh_all, vh_all], axis=1), CONST[...]) + dot_nt(vl_all, CONST[:, 0:128])
        Z[...] = xp.reshape(4, 16, 16, 128)
        c["xp"].start()
        c["xm"].start()

    def turn(value):
        return pltpu.roll(value.reshape(-1, 128), 64, 1).reshape(value.shape)

    def sums_for_other_half(s, c):
        ph, pl_ = split(PART[edge_block])
        for i in range(9):
            m = NMB[edge_block, 3 * i + 2]
            LHO[i, 0:16] = ph * m
            LHO[i, 16:32] = pl_ * m
        sums = dot_nt(LHO[...].reshape(288, 256), WT[edge_block, 0:128]).reshape(9, 32, 128)
        sums = sums[:, 0:16] + sums[:, 16:32]
        LSO[s] = sums[:, 0:8] + turn(sums[:, 8:16])
        neighbours(c, ("ro",), "start", False)

    def sums_for_own_half(s, c):
        for b in range(4):
            ph, pl_ = split(PART[b])
            for i in range(9):
                for pair in range(2):
                    m = NMB[b, 3 * i + pair]
                    LH[2 * i + pair, 0:16, b * 256 : (b + 1) * 256] = ph * m
                    LH[2 * i + pair, 16:32, b * 256 : (b + 1) * 256] = pl_ * m
        sums = None
        for b in range(4):
            lhs = LH[:, :, b * 256 : (b + 1) * 256].reshape(576, 256)
            term = dot_nt(lhs, WT[b, 0:128])
            sums = term if sums is None else sums + term
        sums = sums.reshape(18, 32, 128)
        LSA[s] = (sums[:, 0:16] + sums[:, 16:32]).reshape(9, 2, 16, 128)
        neighbours(c, ("rs",), "start", False)

    def stencil(s, c, first):
        c["xp"].wait_recv()
        c["xm"].wait_recv()
        xr = XR[s]
        xr_h = xr.astype(BF16).astype(F32)
        faces = jnp.concatenate([xr_h, xr - xr_h], axis=0).astype(BF16)
        Z[...] = Z[...] + (dot_tn(faces, edge_1) + dot_tn(faces, edge_2)).reshape(4, 16, 16, 128)
        c["z"].wait_recv()
        when(iy > 0, c["yh"].wait_recv)
        when(iy < 3, c["yl"].wait_recv)
        cur = s + 1
        scale = (1.0 if first else 2.0) / HALF

        def line(i, _):
            o = i // 16
            z = i % 16
            v0 = X[cur, o, z + 4, 8:24, :]
            acc = Z[o, z] + v0 * (POT[z] + (-1.5 * STENCIL[0] - CENTER))
            for k in range(1, 5):
                around = (X[cur, o, z + 4 - k, 8:24, :] + X[cur, o, z + 4 + k, 8:24, :]) + (
                    X[cur, o, z + 4, 8 - k : 24 - k, :] + X[cur, o, z + 4, 8 + k : 24 + k, :]
                )
                acc = acc + (-0.5 * STENCIL[k]) * around
            acc = scale * acc
            Z[o, z] = acc if first else acc - X[s, o, z + 4, 8:24, :]
            return 0

        lax.fori_loop(0, 64, line, 0, unroll=4)

    def scale_totals(s, c, first):
        neighbours(c, ("rs", "ro"), "wait_recv", True)
        total = LSA[s, SELF]
        other = None
        for slot in range(9):
            if slot != SELF:
                total = total + RS[s, slot]
            other = RO[s, slot] if other is None else other + RO[s, slot]
        theirs = lax.broadcasted_iota(I32, (8, 128), 1) // 64 == oz
        other = jnp.concatenate([jnp.where(theirs, other, 0.0), jnp.where(theirs, turn(other), 0.0)], axis=0)
        at_0 = jnp.where(zh == 1, 1.0, 0.0).astype(F32)
        scale = (1.0 if first else 2.0) / HALF
        scaled = scale * SC[...] * jnp.stack([total[0] + at_0 * other, total[1] + (1.0 - at_0) * other])
        CS[s] = scaled
        edge_pair = at_0 * scaled[0] + (1.0 - at_0) * scaled[1]
        CSO[s] = jnp.where(theirs, edge_pair[0:8], turn(edge_pair[8:16]))
        SSA[s, SELF] = scaled
        neighbours(c, ("bo", "bs"), "start", False)

    def take_same(s, c):
        neighbours(c, ("bs",), "wait_recv", True)
        sh, sl = split(SSA[s].reshape(288, 128))
        SHA[:, 0:128] = sh
        SHA[:, 128:256] = sl

    def take_other(s, c):
        neighbours(c, ("bo",), "wait_recv", True)
        packed = SSO[s]
        sh, sl = split(jnp.concatenate([packed, turn(packed)], axis=1).reshape(144, 128))
        SHO[:, 0:128] = sh
        SHO[:, 128:256] = sl

    def per_tile(b, with_other):
        r = dot_nn(SHA[...], WT[b])
        number = NIDX[b]
        pt = jnp.zeros((16, 256), F32)
        for i in range(9):
            for pair in range(2):
                k = 2 * i + pair
                pt = pt + jnp.where(number == 3 * i + pair, r[k * 16 : (k + 1) * 16], 0.0)
        if with_other:
            r = dot_nn(SHO[...], WT[b])
            for i in range(9):
                pt = pt + jnp.where(number == 3 * i + 2, r[i * 16 : (i + 1) * 16], 0.0)
        return pt

    def project(pt, b):
        mask = MKB[b, 0:64]
        results = []
        for o in range(4):
            r = PT[b, 0] * pt[o : o + 1]
            for p in range(1, 4):
                r = r + PT[b, p] * pt[p * 4 + o : p * 4 + o + 1]
            rh, rl = split(r)
            results.append(dot_nt(mask, rh) + dot_nt(mask, rl))
        return jnp.stack(results)

    def apply(s, b, with_other):
        y = Z[:, pl.ds(4 * b, 4)] + project(per_tile(b, with_other), b).reshape(4, 4, 16, 128)
        X[s + 2, :, pl.ds(4 + 4 * b, 4), 8:24, :] = y
        yh, yl = split(y)
        VH[:, pl.ds(4 * b, 4)] = yh
        VL[:, pl.ds(4 * b, 4)] = yl

    c = step_copies(0)
    take_own.wait()
    for v in values:
        v.wait_recv()
    c["z"].start()
    send_y(c)
    for v in parts:
        v.wait_recv()
    sums_for_other_half(0, c)
    sums_for_own_half(0, c)
    for v in cpl_y:
        v.wait_recv()
    group = 2 * (ix * 32)
    cpl_x = [
        start(set_copy(rows(group, 64), rows(group, 64), CP0 + 6 + j, dev((ix + j) % 4, iy, iz))) for j in (1, 3, 2)
    ]
    high, low = split(X[1, :, 4:20, 8:24, :])
    VH[...] = high
    VL[...] = low
    pack_x(0, c)
    for v in cpl_x:
        v.wait_recv()
    home2 = home_in[...]
    home = jnp.concatenate([home2[0:1], home2[1:2]], axis=1)
    home_row = 2 * lax.shift_right_logical(home, 6)
    rows256 = lax.broadcasted_iota(I32, (256, 256), 0)
    lane_hot = jnp.where(row64 == jnp.bitwise_and(home, 63), 1.0, 0.0).astype(F32)
    cb = CB[...]
    cb_1 = cb.astype(BF16)
    rest = cb - cb_1.astype(F32)
    cb_2 = rest.astype(BF16)
    cb_3 = (rest - cb_2.astype(F32)).astype(BF16)
    for r in range(2):
        pick = jnp.where(rows256 == home_row + r, 1.0, 0.0).astype(BF16)
        found = dot_tn(cb_1, pick) + dot_tn(cb_2, pick) + dot_tn(cb_3, pick)
        for p2 in range(2):
            line = jnp.sum(found[p2 * 64 : (p2 + 1) * 64] * lane_hot, axis=0, keepdims=True)
            p = 2 * r + p2
            for pair in range(2):
                SC[pair, p * 4 : (p + 1) * 4, :] = jnp.broadcast_to(line[:, pair * 128 : (pair + 1) * 128], (4, 128))

    scale_totals(0, c, True)

    up[0].wait_recv()
    on_up = start(set_copy(PT.at[below, half[0]], PT.at[below, half[0]], PF0 + 4, ring(1)))
    down[0].wait_recv()
    on_down = start(set_copy(PT.at[above, half[1]], PT.at[above, half[1]], PF0 + 5, ring(3)))
    take_pot.wait()
    for v in pots:
        v.wait_recv()
    stencil(0, c, True)
    def block_sums(b):
        vh = VH[:, pl.ds(4 * b, 4)].reshape(4, 64, 128)
        vl = VL[:, pl.ds(4 * b, 4)].reshape(4, 64, 128)
        tile_sums(vh, vl, b, PART, b)

    def rest_of_step(s, c):
        sums_for_own_half(s, c)
        send_y(c)
        pack_x(s, c)
        scale_totals(s, c, False)
        stencil(s, c, False)

    take_same(0, c)
    take_other(0, c)
    c = step_copies(1)
    for b, arrivals in ((q, ()), (below, (up[1],)), (above, (down[1],)), (across, (on_up, on_down))):
        for v in arrivals:
            v.wait_recv()
        apply(0, b, True)
        block_sums(b)
    c["z"].start()
    sums_for_other_half(1, c)
    rest_of_step(1, c)

    def step(s, _):
        before = step_copies(s - 1)
        c = step_copies(s)
        take_same(s - 1, before)
        take_other(s - 1, before)
        apply(s - 1, edge_block, True)
        c["z"].start()
        block_sums(edge_block)
        sums_for_other_half(s, c)

        def one(j, _):
            b = (edge_block + j) % 4
            apply(s - 1, b, False)
            block_sums(b)
            return 0

        lax.fori_loop(1, 4, one, 0)
        rest_of_step(s, c)
        return 0

    lax.fori_loop(2, STEPS, step, 0)

    last = STEPS - 1
    c = step_copies(last)
    outs_on = around(
        lambda block, o, n: Z.at[pl.ds(o, n), pl.ds(4 * block, 4)],
        lambda block, o, n: ZO.at[pl.ds(4 * block + o, n)],
        RLO,
        OU0,
    )
    take_same(last, c)
    take_other(last, c)
    finals = []
    for j in (2, 1, 3):
        b = (q + j) % 4
        PTS[pl.ds(b, 1)] = per_tile(b, True)[None]
        finals.append(start(set_copy(PTS.at[b], PTR.at[q], FT0 + j - 1, ring(j))))
    outs = outs_on()
    result = Z[:, pl.ds(4 * q, 4)] + project(per_tile(q, True), q).reshape(4, 4, 16, 128)
    out[pl.ds(4 * q, 4)] = result
    for v in outs:
        v.wait_recv()
    for index, j in ((1, 1), (2, 3), (0, 2)):
        finals[index].wait_recv()
        g = (q - j + 4) % 4
        out[pl.ds(4 * g, 4)] = ZO[pl.ds(4 * g, 4)] + project(PTR[g], q).reshape(4, 4, 16, 128)
    for v in sends:
        v.wait_send()

    def drain(s, _):
        c = step_copies(s)
        for name in ("xp", "xm", "z"):
            c[name].wait_send()
        when(iy > 0, c["yl"].wait_send)
        when(iy < 3, c["yh"].wait_send)
        neighbours(c, ("rs", "ro", "bs", "bo"), "wait_send", False)
        return 0

    lax.fori_loop(0, STEPS, drain, 0)


def per_device(orbitals, potential, tile_proj, tile_atom, tile_column, tile_count, atom_home, coupling):
    vmem = pl.BlockSpec(memory_space=pltpu.VMEM)
    hbm = pl.BlockSpec(memory_space=pltpu.HBM)
    smem = pl.BlockSpec(memory_space=pltpu.SMEM)

    def in_hbm(x):
        return pltpu.with_memory_space_constraint(x, pltpu.HBM)

    return pl.pallas_call(
        kernel,
        out_shape=jax.ShapeDtypeStruct((16, 4, 16, 128), F32),
        in_specs=[hbm] * 5 + [smem] + [hbm] * 3,
        out_specs=vmem,
        scratch_shapes=[
            pltpu.VMEM((6, 4, 24, 32, 128), F32),
            pltpu.VMEM((4, 16, 16, 128), F32),
            pltpu.VMEM((4, 16, 16, 128), BF16),
            pltpu.VMEM((4, 16, 16, 128), BF16),
            pltpu.VMEM((1024, 128), F32),
            pltpu.VMEM((4, 4, 128, 256), F32),
            pltpu.VMEM((16, 16, 128), F32),
            pltpu.VMEM((4, 8, 256), I32),
            pltpu.VMEM((4, 128, 256), BF16),
            pltpu.VMEM((4, 16, 256), I32),
            pltpu.VMEM((4, 27, 16, 256), BF16),
            pltpu.VMEM((4, 256, 256), BF16),
            pltpu.VMEM((18, 32, 1024), BF16),
            pltpu.VMEM((9, 32, 256), BF16),
            pltpu.VMEM((4, 9, 2, 16, 128), F32),
            pltpu.VMEM((4, 9, 8, 128), F32),
            pltpu.VMEM((4, 9, 2, 16, 128), F32),
            pltpu.VMEM((4, 9, 8, 128), F32),
            pltpu.VMEM((4, 2, 16, 128), F32),
            pltpu.VMEM((4, 8, 128), F32),
            pltpu.VMEM((4, 9, 2, 16, 128), F32),
            pltpu.VMEM((4, 9, 8, 128), F32),
            pltpu.VMEM((288, 256), BF16),
            pltpu.VMEM((144, 256), BF16),
            pltpu.VMEM((2, 16, 128), F32),
            pltpu.VMEM((4, 8, 1024), F32),
            pltpu.VMEM((4, 8, 1024), F32),
            pltpu.VMEM((256, 128), F32),
            pltpu.VMEM((128, 256), BF16),
            pltpu.VMEM((4, 16, 256), F32),
            pltpu.VMEM((4, 16, 256), F32),
            pltpu.VMEM((4, 16, 256), F32),
            pltpu.VMEM((4, 16, 256), F32),
            pltpu.VMEM((16, 4, 16, 128), F32),
            pltpu.VMEM((16, 4, 16, 128), F32),
            pltpu.VMEM((2, 2, 4, 16, 128), F32),
            pltpu.VMEM((2, 2, 4, 16, 128), F32),
            pltpu.VMEM((1, 256), I32),
            pltpu.VMEM((1, 256), I32),
            pltpu.VMEM((2, 128), I32),
            pltpu.VMEM((4, 64), F32),
            pltpu.VMEM((144, 128), F32),
            pltpu.SemaphoreType.DMA((NSET,)),
            pltpu.SemaphoreType.DMA((NSET,)),
            pltpu.SemaphoreType.DMA((STEPS, NSEM)),
            pltpu.SemaphoreType.DMA((STEPS, NSEM)),
            pltpu.SemaphoreType.DMA((9,)),
        ],
        compiler_params=pltpu.CompilerParams(
            collective_id=0, has_side_effects=True, vmem_limit_bytes=40000 * 1024
        ),
        name="chebyshev",
    )(
        in_hbm(orbitals),
        in_hbm(potential),
        in_hbm(tile_proj.reshape(1024, 128)),
        in_hbm(tile_atom.reshape(1, 256)),
        in_hbm(tile_column.reshape(1, 256)),
        tile_count,
        in_hbm(atom_home.reshape(64, 128)),
        in_hbm(coupling.T),
        in_hbm(jnp.asarray(stencil_constants())),
    )


def solution(mesh):
    return jax.shard_map(
        per_device,
        mesh=mesh,
        in_specs=(
            P(None, "gz", "gy", "gx"),
            P("gz", "gy", "gx"),
            P(("gx", "gy", "gz"), None, None),
            P(("gx", "gy", "gz")),
            P(("gx", "gy", "gz")),
            P(("gx", "gy", "gz")),
            P(),
            P(("gx", "gy", "gz"), None),
        ),
        out_specs=P(None, "gz", "gy", "gx"),
        check_vma=False,
    )
```

profile of v0, /device:TPU:1, one launch (start us, length us, event | category | flops | bytes accessed | tf_op | source)
XLA Modules:
  0.0 82.4 jit_solution(11143636660171483900)
XLA Ops:
  0.7 80.9 %chebyshev.1 = f32[16,4,16,128]{3,2,1,0:T(8,128)S(1)} custom-call(f32[16,4,16,128]{3,2,1,0:T(8,128)} %orb.1, f32[4,16,128]{2,1,0:T(8,128)} %pot_in.1, f32[1024,128]{1,0:T(8,128)} %bitcast.5, s32[1,256]{1,0:T(1,128)} %bitcast.8, s32[1,256]{1,0:T(1,128)} %bitcast.9, s32[1]{0:T(128)S(6)} %copy.11.count_in, s32[64,128]{1,0:T(8,128)} %bitcast.6, ...), custom_call_target="tpu_custom_call" | custom-call | tf_op jit(solution)/shard_map/chebyshev/pallas_call | solution.py:609
  81.6 0.8 copy.12
where the time goes:
time: 82.6 us; the launch traced here: 82.4 us
  Pallas kernels  80.9 us (98%)
    pallas_call x1, Pallas kernels, per_device(): pl.pallas_call(kernel, out_shape=jax.ShapeDtypeStruct((16, 4, 16, 128), F...  80.9 us

commit v1 on v0

--- a/solution.py
+++ b/solution.py
@@ -520,6 +520,7 @@
 
     def rest_of_step(s, c):
         sums_for_own_half(s, c)
+        c["z"].start()
         send_y(c)
         pack_x(s, c)
         scale_totals(s, c, False)
@@ -533,7 +534,6 @@
             v.wait_recv()
         apply(0, b, True)
         block_sums(b)
-    c["z"].start()
     sums_for_other_half(1, c)
     rest_of_step(1, c)
 
@@ -543,7 +543,6 @@
         take_same(s - 1, before)
         take_other(s - 1, before)
         apply(s - 1, edge_block, True)
-        c["z"].start()
         block_sums(edge_block)
         sums_for_other_half(s, c)
 
@@ -567,6 +566,7 @@
         RLO,
         OU0,
     )
+    outs = outs_on()
     take_same(last, c)
     take_other(last, c)
     finals = []
@@ -574,7 +574,6 @@
         b = (q + j) % 4
         PTS[pl.ds(b, 1)] = per_tile(b, True)[None]
         finals.append(start(set_copy(PTS.at[b], PTR.at[q], FT0 + j - 1, ring(j))))
-    outs = outs_on()
     result = Z[:, pl.ds(4 * q, 4)] + project(per_tile(q, True), q).reshape(4, 4, 16, 128)
     out[pl.ds(4 * q, 4)] = result
     for v in outs:

time: 82.6 us -> 85 us (1.029)
  Pallas kernels: 80.9 us -> 83.5 us
    pallas_call x1, Pallas kernels: 80.9 us -> 83.5 us  [per_device(): pl.pallas_call(kernel, out_shape=jax.ShapeDtypeStruct((16, 4, 16, 128), F...]
where the time goes in v1:
time: 85 us; the launch traced here: 84.9 us
  Pallas kernels  83.5 us (98%)
    pallas_call x1, Pallas kernels, per_device(): pl.pallas_call(kernel, out_shape=jax.ShapeDtypeStruct((16, 4, 16, 128), F...  83.5 us

profile of v1, /device:TPU:1, one launch (start us, length us, event | category | flops | bytes accessed | tf_op | source)
XLA Modules:
  0.0 84.9 jit_solution(15971166037849121001)
XLA Ops:
  0.7 83.5 %chebyshev.1 = f32[16,4,16,128]{3,2,1,0:T(8,128)S(1)} custom-call(f32[16,4,16,128]{3,2,1,0:T(8,128)} %orb.1, f32[4,16,128]{2,1,0:T(8,128)} %pot_in.1, f32[1024,128]{1,0:T(8,128)} %bitcast.5, s32[1,256]{1,0:T(1,128)} %bitcast.8, s32[1,256]{1,0:T(1,128)} %bitcast.9, s32[1]{0:T(128)S(6)} %copy.11.count_in, s32[64,128]{1,0:T(8,128)} %bitcast.6, ...), custom_call_target="tpu_custom_call" | custom-call | tf_op jit(solution)/shard_map/chebyshev/pallas_call | solution.py:608
  84.1 0.8 copy.12

commit v2 on v0

--- a/solution.py
+++ b/solution.py
@@ -567,6 +567,7 @@
         RLO,
         OU0,
     )
+    outs = outs_on()
     take_same(last, c)
     take_other(last, c)
     finals = []
@@ -574,7 +575,6 @@
         b = (q + j) % 4
         PTS[pl.ds(b, 1)] = per_tile(b, True)[None]
         finals.append(start(set_copy(PTS.at[b], PTR.at[q], FT0 + j - 1, ring(j))))
-    outs = outs_on()
     result = Z[:, pl.ds(4 * q, 4)] + project(per_tile(q, True), q).reshape(4, 4, 16, 128)
     out[pl.ds(4 * q, 4)] = result
     for v in outs:

time: 82.6 us -> 83.2 us (level); the launches traced: 82.4 us -> 81.9 us
  no operation moved by 1% of the time
where the time goes in v2:
time: 83.2 us; the launch traced here: 81.9 us
  Pallas kernels  80.5 us (97%)
    pallas_call x1, Pallas kernels, per_device(): pl.pallas_call(kernel, out_shape=jax.ShapeDtypeStruct((16, 4, 16, 128), F...  80.5 us

profile of v2, /device:TPU:1, one launch (start us, length us, event | category | flops | bytes accessed | tf_op | source)
XLA Modules:
  0.0 81.9 jit_solution(5950314425548418443)
XLA Ops:
  0.7 80.5 %chebyshev.1 = f32[16,4,16,128]{3,2,1,0:T(8,128)S(1)} custom-call(f32[16,4,16,128]{3,2,1,0:T(8,128)} %orb.1, f32[4,16,128]{2,1,0:T(8,128)} %pot_in.1, f32[1024,128]{1,0:T(8,128)} %bitcast.5, s32[1,256]{1,0:T(1,128)} %bitcast.8, s32[1,256]{1,0:T(1,128)} %bitcast.9, s32[1]{0:T(128)S(6)} %copy.11.count_in, s32[64,128]{1,0:T(8,128)} %bitcast.6, ...), custom_call_target="tpu_custom_call" | custom-call | tf_op jit(solution)/shard_map/chebyshev/pallas_call | solution.py:609
  81.1 0.8 copy.12
